TPU v7x, 256 devices: a whole 4x4x8 slice. The times are simulated.
256 devices in a mesh: pt: 4 (over x_hi, core), ch: 64 (over y, z, x_lo).
Axes of the slice: x: 4 (x_hi: 2, x_lo: 2; x = x_hi * 2 + x_lo), y: 4, z: 8, core: 2. Of those that a mesh axis runs over, the one named last changes fastest.
Arguments:
- voltages: bfloat16 [4096, 2, 64, 2048], P(('pt', 'ch')), parts along dimension 0, may hold values from -6 to 6
- beam_delay: int32 [1024, 64], P('pt'), parts along dimension 0, may hold values from 0 to 4095
- bandpass: float32 [1024], P('ch'), may hold values from 0.4 to 6
- trial_delays: int32 [512, 1024], replicated, may hold values from 0 to 511, as said below
Outputs:
- dedispersed: bfloat16 [2048, 256, 512], P(('pt', 'ch')), parts along dimension 0
There are 4 independent parts, one for each index of `pt`. A program takes and returns all parts, laid end to end along the dimension named above; an argument that names none is the same for every part. Nothing has to cross between parts.
Inputs may be any that keep to these rules, and one draw needn't show every extreme that they name: `trial_delays`: delays are counted in integrated samples.
All inputs are finite; a program needn't handle non-finite values.
Results may differ from a plain program's by a relative error of at most 0.0028.
The roundings to bfloat16 on the way count: a program that leaves them out, or rounds other values in their place, can miss the bound.
Values may be sent and summed in bfloat16 or wider, within the bound.
No kernel may reach another device: no remote copies, remote signals or barrier semaphores. Data moves between devices by JAX's collectives and lax.ppermute only.
A program may use at most 64 MiB of HBM per device.

v0:
```python
import functools
import math
import jax
import jax.numpy as jnp
from jax import lax
from jax.sharding import PartitionSpec as P

CHANNELS = 1024
ANTENNAS = 64
NT = 512
INTEG = 4
NF = 256
two_pi = 2.0 * math.pi
phase_period = 4096


def forward_table():
    sample_index = jnp.arange(NT, dtype=jnp.int32)
    frequencies = jnp.arange(1, NF + 1, dtype=jnp.int32)
    angles = two_pi * (sample_index[:, None] * frequencies[None, :] % NT).astype(jnp.float32) / NT
    return jnp.stack([jnp.cos(angles), -jnp.sin(angles)], axis=1) / math.sqrt(NT)


def inverse_table():
    sample_index = jnp.arange(NT, dtype=jnp.int32)
    frequencies = jnp.arange(1, NF + 1, dtype=jnp.int32)
    angles = two_pi * (frequencies[:, None] * sample_index[None, :] % NT).astype(jnp.float32) / NT
    return (jnp.stack([jnp.cos(angles), -jnp.sin(angles)], axis=1) / math.sqrt(NT)).astype(
        jnp.bfloat16
    )


def weight_block(delays, channel):
    phases = delays * (channel + CHANNELS) % phase_period
    angles = two_pi * phases.astype(jnp.float32) / phase_period
    cosine = jnp.cos(angles)
    sine_part = jnp.sin(angles)
    upper_rows = jnp.concatenate([cosine, sine_part], axis=1)
    lower_rows = jnp.concatenate([-sine_part, cosine], axis=1)
    return (jnp.concatenate([upper_rows, lower_rows], axis=0) / math.sqrt(2 * ANTENNAS)).astype(
        jnp.bfloat16
    )


def channel_power(delays, channel_entry):
    channel, voltage, channel_gain = channel_entry
    weights = weight_block(delays, channel)
    beam_count = delays.shape[0]
    beamformed = jnp.dot(
        weights,
        voltage.reshape(2 * voltage.shape[1], voltage.shape[2]),
        preferred_element_type=jnp.float32,
    )
    squared = beamformed[:beam_count] ** 2 + beamformed[beam_count:] ** 2
    averaged = jnp.mean(squared.reshape(beam_count, squared.shape[1] // INTEG, INTEG), axis=2)
    return averaged * channel_gain


def phasor_block(delays, frequency):
    angles = two_pi * (delays * frequency % NT).astype(jnp.float32) / NT
    cosine = jnp.cos(angles)
    sine_part = jnp.sin(angles)
    upper_rows = jnp.concatenate([cosine, -sine_part], axis=1)
    lower_rows = jnp.concatenate([sine_part, cosine], axis=1)
    return (jnp.concatenate([upper_rows, lower_rows], axis=0) / math.sqrt(CHANNELS)).astype(
        jnp.bfloat16
    )


def shards(voltages, beam_delay, bandpass, trial_delays):
    local_channels = voltages.shape[0]
    position = lax.axis_index("ch")
    channels = position * local_channels + jnp.arange(local_channels, dtype=jnp.int32)
    forward = forward_table()
    backward = inverse_table()
    beam_power = lax.map(
        functools.partial(channel_power, beam_delay), (channels, voltages, bandpass)
    )
    channel_mean = lax.psum(jnp.sum(beam_power, axis=0), "ch") / CHANNELS
    spectra = jnp.einsum(
        "cbt,tkf->kfcb", beam_power - channel_mean, forward, precision=lax.Precision.HIGHEST
    )
    spectra = spectra.astype(jnp.bfloat16)
    spectra_block = lax.all_to_all(spectra, "ch", split_axis=1, concat_axis=2, tiled=True)
    local_freqs = spectra_block.shape[1]

    def one_frequency(freq_index):
        freq_slice = lax.dynamic_index_in_dim(spectra_block, freq_index, 1, keepdims=False)
        phasors = phasor_block(trial_delays, position * local_freqs + freq_index + 1)
        product = jnp.dot(
            phasors,
            freq_slice.reshape(2 * freq_slice.shape[1], freq_slice.shape[2]),
            preferred_element_type=jnp.float32,
        )
        return product.astype(jnp.bfloat16).reshape(2, trial_delays.shape[0], freq_slice.shape[2])

    dedispersed_spectra = lax.map(one_frequency, jnp.arange(local_freqs, dtype=jnp.int32))
    series = jnp.einsum(
        "fkdb,fkt->dbt",
        lax.all_to_all(dedispersed_spectra, "ch", split_axis=2, concat_axis=0, tiled=True),
        backward,
        preferred_element_type=jnp.float32,
    )
    return series.astype(jnp.bfloat16)


def solution(mesh):
    return jax.shard_map(
        shards,
        mesh=mesh,
        in_specs=(P(("pt", "ch"), None, None, None), P("pt", None), P("ch"), P()),
        out_specs=P(("pt", "ch"), None, None),
        check_vma=False,
    )
```

profile of v0, /device:TPU:8, one launch (start us, length us, event | category | flops | bytes accessed | tf_op | source)
XLA Modules:
  0.0 1003.5 jit_solution(11758832814748078061)
XLA Ops:
  6.5 184.7 %while.24 = (s32[]{:T(128)}, f32[16,256,512]{1,2,0:T(8,128)}, s32[16]{0:T(128)S(1)}, s32[256,64]{0,1:T(8,128)}, bf16[16,2,64,2048]{3,2,1,0:T(8,128)(2,1)}, /*ind...) while((s32[]{:T(128)}, f32[16,256,512]{1,2,0:T(8,128)}, s32[16]{0:T(128)S(1)}, ...), condition=%wide.region_2.3_spmd, body=%wide.region_0.2_spmd.sunk | while | flops 271106048 | bytes 24577468 | solution.py:76
  12.9 1.9 reshape.244
  24.4 1.9 reshape.244
  35.9 1.9 reshape.244
  47.5 1.9 reshape.244
  59.0 1.9 reshape.244
  70.6 1.9 reshape.244
  82.1 1.9 reshape.244
  93.7 1.9 reshape.244
  105.2 1.9 reshape.244
  116.7 1.9 reshape.244
  128.3 1.9 reshape.244
  139.8 1.9 reshape.244
  151.4 1.9 reshape.244
  186.0 1.9 reshape.244
  191.3 4.8 reduce_sum.21
  196.1 2.1 fusion.55
  198.2 589.0 %all-reduce.2.cloned.1.call-done = f32[256,512]{0,1:T(8,128)} async-done(((f32[256,512]{0,1:T(8,128)}), f32[256,512]{0,1:T(8,128)}) %all-reduce.2.cloned.1.call-update) | async-done | bytes 524304 | tf_op jit(solution)/shard_map/psum | solution.py:79
  788.3 16.1 %fusion.29 = bf16[2,256,16,256]{3,1,2,0:T(8,128)(2,1)S(1)} fusion(f32[16,256,512]{1,2,0:T(8,128)} %get-tuple-element.165, f32[256,512]{0,1:T(8,128)S(1)} %broadcast_multiply_fusion, f32[512,1,256]{0,2,1:T(8,128)S(1)} %get-tuple-element.200, f32[512,1,256]{0,2,1:T(8,128)S(1)} %get-tuple-element.199), kind=kOutput, calls=%fused_computation.40 | convolution fusion | flops 12889620480 | bytes 14155776 | tf_op jit(solution)/shard_map/cbt,tkf->kfcb/dot_general | solution.py:80
  804.4 4.4 copy.16
  808.7 29.8 %all-to-all-start = ((bf16[2,256,16,256]{3,2,0,1:T(8,128)(2,1)}), bf16[2,256,16,256]{3,2,0,1:T(8,128)(2,1)}, u32[]{:S(2)}, u32[]{:S(2)}) async-start(bf16[2,256,16,256]{3,2,0,1:T(8,128)(2,1)} %copy.16), calls=%async_computation | async-start | bytes 8388608 | tf_op jit(solution)/shard_map/all_to_all | solution.py:84
  838.6 51.6 %all-to-all-done = bf16[2,256,16,256]{3,2,0,1:T(8,128)(2,1)} async-done(((bf16[2,256,16,256]{3,2,0,1:T(8,128)(2,1)}), bf16[2,256,16,256]{3,2,0,1:T(8,128)(2,1)}, u32[]{:S(2)}, u32[]{:S(2)}) %all-to-all-start) | async-done | bytes 4194336 | tf_op jit(solution)/shard_map/all_to_all | solution.py:84
  890.2 4.7 copy.17
  894.9 61.0 %while.25 = (s32[]{:T(128)}, bf16[4,2,512,256]{3,1,0,2:T(2,128)(2,1)}, s32[4]{0:T(128)S(1)}, s32[]{:T(128)}, s32[512,1024]{1,0:T(8,128)S(1)}, /*index=5*/bf16[2,...) while((s32[]{:T(128)}, bf16[4,2,512,256]{3,1,0,2:T(2,128)(2,1)}, s32[4]{0:T(128)S(1)}, s32[]{:T(128)}, ...), condition=%wide.region_6.7_spmd, body=%wide.region_5.6_spmd.sunk | while | flops 1092354048 | bytes 19399340 | solution.py:97
  899.3 8.3 fusion.82
  914.5 8.3 fusion.82
  929.8 8.3 fusion.82
  945.0 8.3 fusion.82
  956.0 7.2 all-to-all-start.1
  963.1 2.1 fusion.54
  965.3 27.6 %all-to-all-done.1 = bf16[4,2,512,256]{3,1,0,2:T(2,128)(2,1)S(1)} async-done(((bf16[4,2,512,256]{3,1,0,2:T(2,128)(2,1)}), bf16[4,2,512,256]{3,1,0,2:T(2,128)(2,1)S(1)}, u32[]{:S(2)}, u32[]{:S(2)}) %all-to-all-start.1) | async-done | bytes 2097184 | tf_op jit(solution)/shard_map/all_to_all | solution.py:100
  993.5 3.1 bitcast_convert_fusion
  (206 shorter events, 156.8 us)
Async XLA Ops:
  6.5 780.7 %all-reduce.2.cloned.1.call-start = ((), (), s32[]{:S(2)}) async-start(), calls=%async_computation.2 | async-start | bytes 1048576 | tf_op jit(solution)/shard_map/psum | solution.py:79
  14.7 1.3 copy-start.1
  26.3 1.3 copy-start.1
  37.8 1.3 copy-start.1
  49.4 1.3 copy-start.1
  60.9 1.3 copy-start.1
  72.4 1.3 copy-start.1
  84.0 1.3 copy-start.1
  95.5 1.3 copy-start.1
  107.1 1.3 copy-start.1
  118.6 1.3 copy-start.1
  130.1 1.3 copy-start.1
  141.7 1.3 copy-start.1
  153.2 1.3 copy-start.1
  164.8 1.3 copy-start.1
  176.3 1.3 copy-start.1
  187.9 1.3 copy-start.1
  808.7 81.5 %all-to-all-start = ((bf16[2,256,16,256]{3,2,0,1:T(8,128)(2,1)}), bf16[2,256,16,256]{3,2,0,1:T(8,128)(2,1)}, u32[]{:S(2)}, u32[]{:S(2)}) async-start(bf16[2,256,16,256]{3,2,0,1:T(8,128)(2,1)} %copy.16), calls=%async_computation | async-start | bytes 8388608 | tf_op jit(solution)/shard_map/all_to_all | solution.py:84
  890.2 4.7 copy-start
  956.0 36.9 %all-to-all-start.1 = ((bf16[4,2,512,256]{3,1,0,2:T(2,128)(2,1)}), bf16[4,2,512,256]{3,1,0,2:T(2,128)(2,1)S(1)}, u32[]{:S(2)}, u32[]{:S(2)}) async-start(bf16[4,2,512,256]{3,1,0,2:T(2,128)(2,1)} %get-tuple-element.166), calls=%async_computation.1 | async-start | bytes 4194304 | tf_op jit(solution)/shard_map/all_to_all | solution.py:100
Sparse Core Ops, SparseCore 0:
  196.2 590.9 all-reduce.1
where the time goes:
time: 1010 us; the launch traced here: 1000 us
  waiting for transfers between devices  668 us (66%)
  local copies, waits for them, and re-layouts  118 us (12%)
  other arithmetic  99.7 us (10%)
  starting transfers between devices  37 us (4%)
  matrix products  36 us (4%)
  loops' own time  31.5 us (3%)
  between operations  13.5 us (1%)
    psum x1, waiting for transfers between devices, shards(): channel_mean = lax.psum(jnp.sum(beam_power, axis=0), 'ch') / CHANNELS  589 us
    all_to_all x1, waiting for transfers between devices, shards(): lax.all_to_all(spectra, 'ch', split_axis=1, concat_axis=2, tiled=True)  51.6 us
    dynamic_slice x48, local copies, waits for them, and re-layouts, shards(): lax.map(functools.partial(channel_power, beam_delay), (channels, voltages...  36.1 us
    neg x4, other arithmetic, phasor_block(): upper_rows = jnp.concatenate([cosine, -sine_part], axis=1)  33.1 us
    all_to_all x1, starting transfers between devices, shards(): lax.all_to_all(spectra, 'ch', split_axis=1, concat_axis=2, tiled=True)  29.8 us
    reshape x16, local copies, waits for them, and re-layouts, channel_power(): squared.reshape(beam_count, squared.shape[1] // INTEG, INTEG)  29.8 us
    add x16, local copies, waits for them, and re-layouts, channel_power(): squared = beamformed[:beam_count] ** 2 + beamformed[beam_count:] ** 2  29 us
    all_to_all x1, waiting for transfers between devices, shards(): lax.all_to_all(dedispersed_spectra, 'ch', split_axis=2, concat_axis=0, ti...  27.6 us
  transfers between devices with their start and end apart: 3, of which 3 were waited for; matrix products, arithmetic and copies ran while one was open for 0% of the time, Pallas kernels for 0%

commit v1 on v0

--- a/solution.py
+++ b/solution.py
@@ -81,7 +81,10 @@
         "cbt,tkf->kfcb", beam_power - channel_mean, forward, precision=lax.Precision.HIGHEST
     )
     spectra = spectra.astype(jnp.bfloat16)
-    spectra_block = lax.all_to_all(spectra, "ch", split_axis=1, concat_axis=2, tiled=True)
+    spectra_block = jnp.concatenate(
+        lax.all_to_all(jnp.stack(jnp.split(spectra, lax.axis_size("ch"), axis=1)), "ch", 0, 0),
+        axis=2,
+    )
     local_freqs = spectra_block.shape[1]
 
     def one_frequency(freq_index):

time: 1010 us -> 1040 us (1.030)
  local copies, waits for them, and re-layouts: 118 us -> 156 us
    unnamed x2 -> x65, local copies, waits for them, and re-layouts: 0.01 us -> 41.3 us
where the time goes in v1:
time: 1040 us
  waiting for transfers between devices  668 us (64%)
  local copies, waits for them, and re-layouts  156 us (15%)
  other arithmetic  99.7 us (10%)
  matrix products  36 us (3%)
  starting transfers between devices  35.1 us (3%)
  loops' own time  31.4 us (3%)
  between operations  13.5 us (1%)
    psum x1, waiting for transfers between devices, shards(): channel_mean = lax.psum(jnp.sum(beam_power, axis=0), 'ch') / CHANNELS  589 us
    all_to_all x1, waiting for transfers between devices, shards(): lax.all_to_all(jnp.stack(jnp.split(spectra, lax.axis_size('ch'), axis=1))...  51.6 us
    unnamed x65, local copies, waits for them, and re-layouts  41.3 us
    dynamic_slice x48, local copies, waits for them, and re-layouts, shards(): lax.map(functools.partial(channel_power, beam_delay), (channels, voltages...  36.1 us
    neg x4, other arithmetic, phasor_block(): upper_rows = jnp.concatenate([cosine, -sine_part], axis=1)  33.1 us
    reshape x16, local copies, waits for them, and re-layouts, channel_power(): squared.reshape(beam_count, squared.shape[1] // INTEG, INTEG)  30 us
    add x16, local copies, waits for them, and re-layouts, channel_power(): squared = beamformed[:beam_count] ** 2 + beamformed[beam_count:] ** 2  29 us
    all_to_all x1, starting transfers between devices, shards(): lax.all_to_all(jnp.stack(jnp.split(spectra, lax.axis_size('ch'), axis=1))...  27.9 us
  transfers between devices with their start and end apart: 3, of which 3 were waited for; matrix products, arithmetic and copies ran while one was open for 0% of the time, Pallas kernels for 0%

profile of v1, /device:TPU:8, one launch (start us, length us, event | category | flops | bytes accessed | tf_op | source)
XLA Modules:
  0.0 1039.5 jit_solution(11208466498092350806)
XLA Ops:
  6.5 184.8 %while.24 = (s32[]{:T(128)}, f32[16,256,512]{1,2,0:T(8,128)}, s32[16]{0:T(128)S(1)}, s32[256,64]{0,1:T(8,128)}, bf16[16,2,64,2048]{3,2,1,0:T(8,128)(2,1)}, /*ind...) while((s32[]{:T(128)}, f32[16,256,512]{1,2,0:T(8,128)}, s32[16]{0:T(128)S(1)}, ...), condition=%wide.region_2.3_spmd, body=%wide.region_0.2_spmd.sunk | while | flops 271106048 | bytes 24577468 | solution.py:76
  12.9 1.9 reshape.252
  24.4 1.9 reshape.252
  35.9 1.9 reshape.252
  47.5 1.9 reshape.252
  59.0 1.9 reshape.252
  70.6 1.9 reshape.252
  82.1 1.9 reshape.252
  93.7 1.9 reshape.252
  105.2 1.9 reshape.252
  116.8 1.9 reshape.252
  128.3 1.9 reshape.252
  139.9 1.9 reshape.252
  163.0 1.9 reshape.252
  174.5 1.9 reshape.252
  186.0 1.9 reshape.252
  191.3 4.8 reduce_sum.21
  196.1 2.1 fusion.55
  198.3 589.0 %all-reduce.2.cloned.1.call-done = f32[256,512]{0,1:T(8,128)} async-done(((f32[256,512]{0,1:T(8,128)}), f32[256,512]{0,1:T(8,128)}) %all-reduce.2.cloned.1.call-update) | async-done | bytes 524304 | tf_op jit(solution)/shard_map/psum | solution.py:79
  788.3 16.1 %fusion.29 = bf16[2,256,16,256]{3,1,2,0:T(8,128)(2,1)S(1)} fusion(f32[16,256,512]{1,2,0:T(8,128)} %get-tuple-element.165, f32[256,512]{0,1:T(8,128)S(1)} %broadcast_multiply_fusion, f32[512,1,256]{0,2,1:T(8,128)S(1)} %get-tuple-element.200, f32[512,1,256]{0,2,1:T(8,128)S(1)} %get-tuple-element.199), kind=kOutput, calls=%fused_computation.40 | convolution fusion | flops 12889620480 | bytes 14155776 | tf_op jit(solution)/shard_map/cbt,tkf->kfcb/dot_general | solution.py:80
  846.4 27.9 %all-to-all-start = ((bf16[64,2,4,16,256]{4,2,3,1,0:T(4,128)(2,1)}), bf16[64,2,4,16,256]{4,2,3,1,0:T(4,128)(2,1)}, u32[]{:S(2)}, u32[]{:S(2)}) async-start(bf16[64,2,4,16,256]{4,2,3,1,0:T(4,128)(2,1)} %constant_dynamic-update-slice_fusion), calls=%async_computation | async-start | bytes 8388608 | tf_op jit(solution)/shard_map/all_to_all | solution.py:85
  874.4 51.6 %all-to-all-done = bf16[64,2,4,16,256]{4,2,3,1,0:T(4,128)(2,1)} async-done(((bf16[64,2,4,16,256]{4,2,3,1,0:T(4,128)(2,1)}), bf16[64,2,4,16,256]{4,2,3,1,0:T(4,128)(2,1)}, u32[]{:S(2)}, u32[]{:S(2)}) %all-to-all-start) | async-done | bytes 4194336 | tf_op jit(solution)/shard_map/all_to_all | solution.py:85
  926.0 4.9 copy.15
  930.9 61.0 %while.25 = (s32[]{:T(128)}, bf16[4,2,512,256]{3,1,0,2:T(2,128)(2,1)}, s32[4]{0:T(128)S(1)}, s32[]{:T(128)}, s32[512,1024]{1,0:T(8,128)S(1)}, /*index=5*/bf16[2,...) while((s32[]{:T(128)}, bf16[4,2,512,256]{3,1,0,2:T(2,128)(2,1)}, s32[4]{0:T(128)S(1)}, s32[]{:T(128)}, ...), condition=%wide.region_6.7_spmd, body=%wide.region_5.6_spmd.sunk | while | flops 1092354048 | bytes 19399340 | solution.py:100
  935.3 8.3 fusion.82
  950.5 8.3 fusion.82
  965.8 8.3 fusion.82
  981.0 8.3 fusion.82
  991.9 7.2 all-to-all-start.1
  999.2 2.1 fusion.54
  1001.3 27.6 %all-to-all-done.1 = bf16[4,2,512,256]{3,1,0,2:T(2,128)(2,1)S(1)} async-done(((bf16[4,2,512,256]{3,1,0,2:T(2,128)(2,1)}), bf16[4,2,512,256]{3,1,0,2:T(2,128)(2,1)S(1)}, u32[]{:S(2)}, u32[]{:S(2)}) %all-to-all-start.1) | async-done | bytes 2097184 | tf_op jit(solution)/shard_map/all_to_all | solution.py:103
  1029.6 3.1 bitcast_convert_fusion
  (269 shorter events, 196.9 us)
Async XLA Ops:
  6.5 780.7 %all-reduce.2.cloned.1.call-start = ((), (), s32[]{:S(2)}) async-start(), calls=%async_computation.2 | async-start | bytes 1048576 | tf_op jit(solution)/shard_map/psum | solution.py:79
  12.9 3.1 copy-start.1
  24.4 3.1 copy-start.1
  35.9 3.1 copy-start.1
  47.5 3.1 copy-start.1
  59.0 3.1 copy-start.1
  70.6 3.1 copy-start.1
  82.1 3.1 copy-start.1
  93.7 3.1 copy-start.1
  105.2 3.1 copy-start.1
  116.8 3.1 copy-start.1
  128.3 3.1 copy-start.1
  139.9 3.1 copy-start.1
  151.4 3.1 copy-start.1
  163.0 3.1 copy-start.1
  174.5 3.1 copy-start.1
  186.0 3.1 copy-start.1
  846.4 79.6 %all-to-all-start = ((bf16[64,2,4,16,256]{4,2,3,1,0:T(4,128)(2,1)}), bf16[64,2,4,16,256]{4,2,3,1,0:T(4,128)(2,1)}, u32[]{:S(2)}, u32[]{:S(2)}) async-start(bf16[64,2,4,16,256]{4,2,3,1,0:T(4,128)(2,1)} %constant_dynamic-update-slice_fusion), calls=%async_computation | async-start | bytes 8388608 | tf_op jit(solution)/shard_map/all_to_all | solution.py:85
  926.0 4.9 copy-start
  991.9 36.9 %all-to-all-start.1 = ((bf16[4,2,512,256]{3,1,0,2:T(2,128)(2,1)}), bf16[4,2,512,256]{3,1,0,2:T(2,128)(2,1)S(1)}, u32[]{:S(2)}, u32[]{:S(2)}) async-start(bf16[4,2,512,256]{3,1,0,2:T(2,128)(2,1)} %get-tuple-element.166), calls=%async_computation.1 | async-start | bytes 4194304 | tf_op jit(solution)/shard_map/all_to_all | solution.py:103
Sparse Core Ops, SparseCore 0:
  196.2 590.9 all-reduce.1
